TPU v7x, 32 devices: a whole 2x2x4 slice. The times are simulated.
32 devices in a mesh: row: 8 (over z, x), col: 4 (over y, core).
Axes of the slice: x: 2, y: 2, z: 4, core: 2. Of those that a mesh axis runs over, the one named last changes fastest.
Arguments:
- vectors: float32 [8192, 1024], P(('row', 'col')), may hold values from -6 to 6
- rotation: float32 [1024, 1024], P(None, 'col'), may hold values from -0.1875 to 0.1875
- blocks: bfloat16 [64, 16, 128, 128], P('row'), may hold values from -0.0625 to 0.0625
- cols: int32 [64, 16], P('row'), may hold values from 0 to 15, as said below
- lists: int32 [8, 2, 4], P('row'), may hold values from 0 to 7, as said below
- counts: int32 [8], P('row'), may hold values from 4 to 8, as said below
Outputs:
- filtered: float32 [1024, 8192], P('col', 'row')
Inputs may be any that keep to these rules, and one draw needn't show every extreme that they name: `counts`: at least one group uses all 8 slots. Every entry of lists[r] is below counts[r], and lists[r, j, 0] = counts[r] - 1; entries may repeat. cols[t, 0] = 4 + t % 8, the block row itself; on valid block rows of group r every slot between 4 and 15 that names an own block row is below 4 + counts[r].
All inputs are finite; a program needn't handle non-finite values.
Results may differ from a plain program's by a relative error of at most 0.0065.
Values may be sent and summed in bfloat16 or wider, within the bound.
No kernel may reach another device: no remote copies, remote signals or barrier semaphores. Data moves between devices by JAX's collectives and lax.ppermute only.
A program may use at most 64 MiB of HBM per device.

v0:
```python
import jax
import jax.numpy as jnp
from jax import lax
from jax.sharding import PartitionSpec as P

STEPS = 10


def passed_along(x, axis, by):
    length = lax.axis_size(axis)
    pairs = [(i, i + by) for i in range(length) if 0 <= i + by < length]
    return lax.ppermute(x, axis, pairs)


def apply_blocks(field, blocks, cols, lists, valid):
    lowered = field.astype(jnp.bfloat16)
    up_rows = lowered[:, lists[0, 0], :]
    down_rows = lowered[:, lists[0, 1], :]
    from_prev = passed_along(up_rows, "row", 1)
    from_next = passed_along(down_rows, "row", -1)
    source = jnp.concatenate([from_prev, lowered, from_next], axis=1)
    picked = source[:, cols, :]
    result = jnp.einsum("cbkj,bkij->cbi", picked, blocks, preferred_element_type=jnp.float32)
    return result * valid[None, :, None]


def body(vectors, rotation, blocks, cols, lists, counts):
    cap = blocks.shape[0]
    width = blocks.shape[2]
    panel = lax.dot_general(
        rotation,
        lax.all_gather(vectors, "col", axis=0, tiled=True),
        (((0,), (1,)), ((), ())),
        precision=lax.Precision.HIGHEST,
        preferred_element_type=jnp.float32,
    )
    panel_cols = panel.shape[0]
    valid = (jnp.arange(cap, dtype=jnp.int32) < counts[0]).astype(jnp.float32)
    previous = panel.reshape(panel_cols, cap, width) * valid[None, :, None]
    current = apply_blocks(previous, blocks, cols, lists, valid)

    def advance(index, carry):
        older, newer = carry
        return (newer, 2.0 * apply_blocks(newer, blocks, cols, lists, valid) - older)

    previous, current = lax.fori_loop(0, STEPS - 1, advance, (previous, current))
    return current.reshape(panel_cols, cap * width)


def solution(mesh):
    return jax.shard_map(
        body,
        mesh=mesh,
        in_specs=(
            P(("row", "col"), None),
            P(None, "col"),
            P("row", None, None, None),
            P("row", None),
            P("row", None, None),
            P("row"),
        ),
        out_specs=P("col", "row"),
        check_vma=False,
    )
```

profile of v0, /device:TPU:0, one launch (start us, length us, event | category | flops | bytes accessed | tf_op | source)
XLA Modules:
  0.0 394.8 jit_solution(11017136291069954017)
XLA Ops:
  8.7 37.4 %all-gather.2.cloned.1.call-done = f32[1024,1024]{1,0:T(8,128)} async-done(((f32[256,1024]{1,0:T(8,128)}), f32[1024,1024]{1,0:T(8,128)}) %all-gather.2.cloned.1.call-update) | async-done | bytes 4194320 | tf_op jit(solution)/shard_map/all_gather | solution.py:32
  46.1 8.7 %convolution_bitcast_fusion.2 = f32[32,8,8,128]{3,2,1,0:T(8,128)S(1)} fusion(f32[1024,256]{1,0:T(8,128)S(1)} %copy-done, f32[1024,1024]{1,0:T(8,128)} %all-gather.2.cloned.1.call-done), kind=kOutput, calls=%fused_computation.25 | convolution fusion | flops 3221225472 | bytes 6291456 | tf_op jit(solution)/shard_map/dot_general | solution.py:30
  56.7 3.4 collective-permute-start.2
  60.7 1.3 collective-permute-start.3
  62.1 9.5 %collective-permute-done.2 = bf16[256,4,128]{2,0,1:T(8,128)(2,1)S(1)} collective-permute-done((bf16[256,4,128]{2,0,1:T(8,128)(2,1)S(1)}, bf16[256,4,128]{2,0,1:T(8,128)(2,1)S(1)}, u32[]{:S(2)}, u32[]{:S(2)}) %collective-permute-start.2) | collective-permute-done | bytes 262176 | tf_op jit(solution)/shard_map/ppermute | solution.py:12
  71.7 6.6 %gather_fusion.5 = bf16[128,256,128]{2,1,0:T(8,128)(2,1)} fusion(bf16[256,16,128]{2,0,1:T(8,128)(2,1)S(1)} %pad_maximum_fusion.1, s32[1024]{0:T(1024)S(1)} %pad_clamp_fusion.3), kind=kCustom, calls=%fused_computation.5 | custom fusion | bytes 16777728 | tf_op jit(solution)/shard_map/gather | solution.py:22
  78.3 6.9 %fusion.9 = f32[256,8,128]{2,0,1:T(8,128)S(1)} fusion(bf16[256,8,16,128]{3,0,2,1:T(8,128)(2,1)} %bitcast.93, bf16[8,16,128,128]{3,2,1,0:T(8,128)(2,1)} %param.10, f32[8]{0:T(128)S(1)} %compare_convert_fusion.1), kind=kOutput, calls=%fused_computation.24 | convolution fusion | flops 1074003968 | bytes 13631520 | tf_op jit(solution)/shard_map/cbkj,bkij->cbi/dot_general | solution.py:23
  85.2 301.6 %while.13 = (s32[]{:T(128)}, f32[256,8,128]{2,0,1:T(8,128)}, f32[256,8,128]{2,0,1:T(8,128)S(1)}, s32[1,2,4]{2,1,0:T(2,128)S(1)}, s32[8,16]{1,0:T(8,128)S(1)}, /*...) while((s32[]{:T(128)}, f32[256,8,128]{2,0,1:T(8,128)}, f32[256,8,128]{2,0,1:T(8,128)S(1)}, ...), condition=%wide.region_1.0_spmd.clone, body=%wide.region_0.0_spmd.clone.sunk | while | flops 1075842432 | bytes 44580228 | solution.py:46
  86.0 1.3 collective-permute-start
  87.9 5.7 %collective-permute-start.1 = (bf16[256,4,128]{2,0,1:T(8,128)(2,1)S(1)}, bf16[256,4,128]{2,0,1:T(8,128)(2,1)}, u32[]{:S(2)}, u32[]{:S(2)}) collective-permute-start(bf16[256,4,128]{2,0,1:T(8,128)(2,1)S(1)} %bitcast.95), channel_id=1, source_target_pairs={{0,4},{4,8},{8,12},{12,16},{16,20},{20,24},{24,28},{1,5},{5,9},{9,... | collective-permute-start | bytes 786440 | tf_op jit(solution)/shard_map/while/body/eval_jaxpr/ppermute | solution.py:12
  94.4 1.8 collective-permute-done
  96.2 6.1 %collective-permute-done.1 = bf16[256,4,128]{2,0,1:T(8,128)(2,1)} collective-permute-done((bf16[256,4,128]{2,0,1:T(8,128)(2,1)S(1)}, bf16[256,4,128]{2,0,1:T(8,128)(2,1)}, u32[]{:S(2)}, u32[]{:S(2)}) %collective-permute-start.1) | collective-permute-done | bytes 262176 | tf_op jit(solution)/shard_map/while/body/eval_jaxpr/ppermute | solution.py:12
  103.6 6.6 %gather_fusion.2 = bf16[128,256,128]{2,1,0:T(8,128)(2,1)} fusion(bf16[256,16,128]{2,0,1:T(8,128)(2,1)S(1)} %pad_maximum_fusion.3, s32[1024]{0:T(1024)S(1)} %pad_clamp_fusion.9), kind=kCustom, calls=%fused_computation.2.clone.clone.1 | custom fusion | bytes 16777728 | tf_op jit(solution)/shard_map/while/body/eval_jaxpr/gather | solution.py:22
  110.2 7.2 %fusion.27 = f32[256,8,128]{2,0,1:T(8,128)S(1)} fusion(f32[256,8,128]{2,0,1:T(8,128)} %get-tuple-element.144, bf16[256,8,16,128]{3,0,2,1:T(8,128)(2,1)} %bitcast.92, bf16[8,16,128,128]{3,2,1,0:T(8,128)(2,1)} %get-tuple-element.156, f32[8]{0:T(128)S(1)} %compare_convert_fusion.3), kind=kOutput, calls=%fused_computation.11.clone.1 | convolution fusion | flops 1074528256 | bytes 14680096 | tf_op jit(solution)/shard_map/while/body/eval_jaxpr/cbkj,bkij->cbi/dot_general | solution.py:23
  119.1 1.3 collective-permute-start
  121.1 5.8 %collective-permute-start.1 = (bf16[256,4,128]{2,0,1:T(8,128)(2,1)S(1)}, bf16[256,4,128]{2,0,1:T(8,128)(2,1)}, u32[]{:S(2)}, u32[]{:S(2)}) collective-permute-start(bf16[256,4,128]{2,0,1:T(8,128)(2,1)S(1)} %bitcast.95), channel_id=1, source_target_pairs={{0,4},{4,8},{8,12},{12,16},{16,20},{20,24},{24,28},{1,5},{5,9},{9,... | collective-permute-start | bytes 786440 | tf_op jit(solution)/shard_map/while/body/eval_jaxpr/ppermute | solution.py:12
  127.6 2.5 collective-permute-done
  130.1 5.8 %collective-permute-done.1 = bf16[256,4,128]{2,0,1:T(8,128)(2,1)} collective-permute-done((bf16[256,4,128]{2,0,1:T(8,128)(2,1)S(1)}, bf16[256,4,128]{2,0,1:T(8,128)(2,1)}, u32[]{:S(2)}, u32[]{:S(2)}) %collective-permute-start.1) | collective-permute-done | bytes 262176 | tf_op jit(solution)/shard_map/while/body/eval_jaxpr/ppermute | solution.py:12
  137.1 6.6 %gather_fusion.2 = bf16[128,256,128]{2,1,0:T(8,128)(2,1)} fusion(bf16[256,16,128]{2,0,1:T(8,128)(2,1)S(1)} %pad_maximum_fusion.3, s32[1024]{0:T(1024)S(1)} %pad_clamp_fusion.9), kind=kCustom, calls=%fused_computation.2.clone.clone.1 | custom fusion | bytes 16777728 | tf_op jit(solution)/shard_map/while/body/eval_jaxpr/gather | solution.py:22
  143.7 7.2 %fusion.27 = f32[256,8,128]{2,0,1:T(8,128)S(1)} fusion(f32[256,8,128]{2,0,1:T(8,128)} %get-tuple-element.144, bf16[256,8,16,128]{3,0,2,1:T(8,128)(2,1)} %bitcast.92, bf16[8,16,128,128]{3,2,1,0:T(8,128)(2,1)} %get-tuple-element.156, f32[8]{0:T(128)S(1)} %compare_convert_fusion.3), kind=kOutput, calls=%fused_computation.11.clone.1 | convolution fusion | flops 1074528256 | bytes 14680096 | tf_op jit(solution)/shard_map/while/body/eval_jaxpr/cbkj,bkij->cbi/dot_general | solution.py:23
  152.7 1.3 collective-permute-start
  154.6 5.8 %collective-permute-start.1 = (bf16[256,4,128]{2,0,1:T(8,128)(2,1)S(1)}, bf16[256,4,128]{2,0,1:T(8,128)(2,1)}, u32[]{:S(2)}, u32[]{:S(2)}) collective-permute-start(bf16[256,4,128]{2,0,1:T(8,128)(2,1)S(1)} %bitcast.95), channel_id=1, source_target_pairs={{0,4},{4,8},{8,12},{12,16},{16,20},{20,24},{24,28},{1,5},{5,9},{9,... | collective-permute-start | bytes 786440 | tf_op jit(solution)/shard_map/while/body/eval_jaxpr/ppermute | solution.py:12
  161.2 2.5 collective-permute-done
  163.7 5.8 %collective-permute-done.1 = bf16[256,4,128]{2,0,1:T(8,128)(2,1)} collective-permute-done((bf16[256,4,128]{2,0,1:T(8,128)(2,1)S(1)}, bf16[256,4,128]{2,0,1:T(8,128)(2,1)}, u32[]{:S(2)}, u32[]{:S(2)}) %collective-permute-start.1) | collective-permute-done | bytes 262176 | tf_op jit(solution)/shard_map/while/body/eval_jaxpr/ppermute | solution.py:12
  170.7 6.6 %gather_fusion.2 = bf16[128,256,128]{2,1,0:T(8,128)(2,1)} fusion(bf16[256,16,128]{2,0,1:T(8,128)(2,1)S(1)} %pad_maximum_fusion.3, s32[1024]{0:T(1024)S(1)} %pad_clamp_fusion.9), kind=kCustom, calls=%fused_computation.2.clone.clone.1 | custom fusion | bytes 16777728 | tf_op jit(solution)/shard_map/while/body/eval_jaxpr/gather | solution.py:22
  177.2 7.2 %fusion.27 = f32[256,8,128]{2,0,1:T(8,128)S(1)} fusion(f32[256,8,128]{2,0,1:T(8,128)} %get-tuple-element.144, bf16[256,8,16,128]{3,0,2,1:T(8,128)(2,1)} %bitcast.92, bf16[8,16,128,128]{3,2,1,0:T(8,128)(2,1)} %get-tuple-element.156, f32[8]{0:T(128)S(1)} %compare_convert_fusion.3), kind=kOutput, calls=%fused_computation.11.clone.1 | convolution fusion | flops 1074528256 | bytes 14680096 | tf_op jit(solution)/shard_map/while/body/eval_jaxpr/cbkj,bkij->cbi/dot_general | solution.py:23
  186.2 1.3 collective-permute-start
  188.2 5.8 %collective-permute-start.1 = (bf16[256,4,128]{2,0,1:T(8,128)(2,1)S(1)}, bf16[256,4,128]{2,0,1:T(8,128)(2,1)}, u32[]{:S(2)}, u32[]{:S(2)}) collective-permute-start(bf16[256,4,128]{2,0,1:T(8,128)(2,1)S(1)} %bitcast.95), channel_id=1, source_target_pairs={{0,4},{4,8},{8,12},{12,16},{16,20},{20,24},{24,28},{1,5},{5,9},{9,... | collective-permute-start | bytes 786440 | tf_op jit(solution)/shard_map/while/body/eval_jaxpr/ppermute | solution.py:12
  194.7 2.5 collective-permute-done
  197.2 5.8 %collective-permute-done.1 = bf16[256,4,128]{2,0,1:T(8,128)(2,1)} collective-permute-done((bf16[256,4,128]{2,0,1:T(8,128)(2,1)S(1)}, bf16[256,4,128]{2,0,1:T(8,128)(2,1)}, u32[]{:S(2)}, u32[]{:S(2)}) %collective-permute-start.1) | collective-permute-done | bytes 262176 | tf_op jit(solution)/shard_map/while/body/eval_jaxpr/ppermute | solution.py:12
  204.2 6.6 %gather_fusion.2 = bf16[128,256,128]{2,1,0:T(8,128)(2,1)} fusion(bf16[256,16,128]{2,0,1:T(8,128)(2,1)S(1)} %pad_maximum_fusion.3, s32[1024]{0:T(1024)S(1)} %pad_clamp_fusion.9), kind=kCustom, calls=%fused_computation.2.clone.clone.1 | custom fusion | bytes 16777728 | tf_op jit(solution)/shard_map/while/body/eval_jaxpr/gather | solution.py:22
  210.8 7.2 %fusion.27 = f32[256,8,128]{2,0,1:T(8,128)S(1)} fusion(f32[256,8,128]{2,0,1:T(8,128)} %get-tuple-element.144, bf16[256,8,16,128]{3,0,2,1:T(8,128)(2,1)} %bitcast.92, bf16[8,16,128,128]{3,2,1,0:T(8,128)(2,1)} %get-tuple-element.156, f32[8]{0:T(128)S(1)} %compare_convert_fusion.3), kind=kOutput, calls=%fused_computation.11.clone.1 | convolution fusion | flops 1074528256 | bytes 14680096 | tf_op jit(solution)/shard_map/while/body/eval_jaxpr/cbkj,bkij->cbi/dot_general | solution.py:23
  219.8 1.3 collective-permute-start
  221.7 5.8 %collective-permute-start.1 = (bf16[256,4,128]{2,0,1:T(8,128)(2,1)S(1)}, bf16[256,4,128]{2,0,1:T(8,128)(2,1)}, u32[]{:S(2)}, u32[]{:S(2)}) collective-permute-start(bf16[256,4,128]{2,0,1:T(8,128)(2,1)S(1)} %bitcast.95), channel_id=1, source_target_pairs={{0,4},{4,8},{8,12},{12,16},{16,20},{20,24},{24,28},{1,5},{5,9},{9,... | collective-permute-start | bytes 786440 | tf_op jit(solution)/shard_map/while/body/eval_jaxpr/ppermute | solution.py:12
  228.3 2.5 collective-permute-done
  230.8 5.8 %collective-permute-done.1 = bf16[256,4,128]{2,0,1:T(8,128)(2,1)} collective-permute-done((bf16[256,4,128]{2,0,1:T(8,128)(2,1)S(1)}, bf16[256,4,128]{2,0,1:T(8,128)(2,1)}, u32[]{:S(2)}, u32[]{:S(2)}) %collective-permute-start.1) | collective-permute-done | bytes 262176 | tf_op jit(solution)/shard_map/while/body/eval_jaxpr/ppermute | solution.py:12
  237.8 6.6 %gather_fusion.2 = bf16[128,256,128]{2,1,0:T(8,128)(2,1)} fusion(bf16[256,16,128]{2,0,1:T(8,128)(2,1)S(1)} %pad_maximum_fusion.3, s32[1024]{0:T(1024)S(1)} %pad_clamp_fusion.9), kind=kCustom, calls=%fused_computation.2.clone.clone.1 | custom fusion | bytes 16777728 | tf_op jit(solution)/shard_map/while/body/eval_jaxpr/gather | solution.py:22
  244.3 7.2 %fusion.27 = f32[256,8,128]{2,0,1:T(8,128)S(1)} fusion(f32[256,8,128]{2,0,1:T(8,128)} %get-tuple-element.144, bf16[256,8,16,128]{3,0,2,1:T(8,128)(2,1)} %bitcast.92, bf16[8,16,128,128]{3,2,1,0:T(8,128)(2,1)} %get-tuple-element.156, f32[8]{0:T(128)S(1)} %compare_convert_fusion.3), kind=kOutput, calls=%fused_computation.11.clone.1 | convolution fusion | flops 1074528256 | bytes 14680096 | tf_op jit(solution)/shard_map/while/body/eval_jaxpr/cbkj,bkij->cbi/dot_general | solution.py:23
  253.3 1.3 collective-permute-start
  255.3 5.8 %collective-permute-start.1 = (bf16[256,4,128]{2,0,1:T(8,128)(2,1)S(1)}, bf16[256,4,128]{2,0,1:T(8,128)(2,1)}, u32[]{:S(2)}, u32[]{:S(2)}) collective-permute-start(bf16[256,4,128]{2,0,1:T(8,128)(2,1)S(1)} %bitcast.95), channel_id=1, source_target_pairs={{0,4},{4,8},{8,12},{12,16},{16,20},{20,24},{24,28},{1,5},{5,9},{9,... | collective-permute-start | bytes 786440 | tf_op jit(solution)/shard_map/while/body/eval_jaxpr/ppermute | solution.py:12
  261.8 2.5 collective-permute-done
  264.3 5.8 %collective-permute-done.1 = bf16[256,4,128]{2,0,1:T(8,128)(2,1)} collective-permute-done((bf16[256,4,128]{2,0,1:T(8,128)(2,1)S(1)}, bf16[256,4,128]{2,0,1:T(8,128)(2,1)}, u32[]{:S(2)}, u32[]{:S(2)}) %collective-permute-start.1) | collective-permute-done | bytes 262176 | tf_op jit(solution)/shard_map/while/body/eval_jaxpr/ppermute | solution.py:12
  271.3 6.6 %gather_fusion.2 = bf16[128,256,128]{2,1,0:T(8,128)(2,1)} fusion(bf16[256,16,128]{2,0,1:T(8,128)(2,1)S(1)} %pad_maximum_fusion.3, s32[1024]{0:T(1024)S(1)} %pad_clamp_fusion.9), kind=kCustom, calls=%fused_computation.2.clone.clone.1 | custom fusion | bytes 16777728 | tf_op jit(solution)/shard_map/while/body/eval_jaxpr/gather | solution.py:22
  277.9 7.2 %fusion.27 = f32[256,8,128]{2,0,1:T(8,128)S(1)} fusion(f32[256,8,128]{2,0,1:T(8,128)} %get-tuple-element.144, bf16[256,8,16,128]{3,0,2,1:T(8,128)(2,1)} %bitcast.92, bf16[8,16,128,128]{3,2,1,0:T(8,128)(2,1)} %get-tuple-element.156, f32[8]{0:T(128)S(1)} %compare_convert_fusion.3), kind=kOutput, calls=%fused_computation.11.clone.1 | convolution fusion | flops 1074528256 | bytes 14680096 | tf_op jit(solution)/shard_map/while/body/eval_jaxpr/cbkj,bkij->cbi/dot_general | solution.py:23
  286.9 1.3 collective-permute-start
  288.8 5.8 %collective-permute-start.1 = (bf16[256,4,128]{2,0,1:T(8,128)(2,1)S(1)}, bf16[256,4,128]{2,0,1:T(8,128)(2,1)}, u32[]{:S(2)}, u32[]{:S(2)}) collective-permute-start(bf16[256,4,128]{2,0,1:T(8,128)(2,1)S(1)} %bitcast.95), channel_id=1, source_target_pairs={{0,4},{4,8},{8,12},{12,16},{16,20},{20,24},{24,28},{1,5},{5,9},{9,... | collective-permute-start | bytes 786440 | tf_op jit(solution)/shard_map/while/body/eval_jaxpr/ppermute | solution.py:12
  295.4 2.5 collective-permute-done
  297.9 5.8 %collective-permute-done.1 = bf16[256,4,128]{2,0,1:T(8,128)(2,1)} collective-permute-done((bf16[256,4,128]{2,0,1:T(8,128)(2,1)S(1)}, bf16[256,4,128]{2,0,1:T(8,128)(2,1)}, u32[]{:S(2)}, u32[]{:S(2)}) %collective-permute-start.1) | collective-permute-done | bytes 262176 | tf_op jit(solution)/shard_map/while/body/eval_jaxpr/ppermute | solution.py:12
  303.7 1.2 pad_maximum_fusion.3
  304.9 6.6 %gather_fusion.2 = bf16[128,256,128]{2,1,0:T(8,128)(2,1)} fusion(bf16[256,16,128]{2,0,1:T(8,128)(2,1)S(1)} %pad_maximum_fusion.3, s32[1024]{0:T(1024)S(1)} %pad_clamp_fusion.9), kind=kCustom, calls=%fused_computation.2.clone.clone.1 | custom fusion | bytes 16777728 | tf_op jit(solution)/shard_map/while/body/eval_jaxpr/gather | solution.py:22
  311.5 7.2 %fusion.27 = f32[256,8,128]{2,0,1:T(8,128)S(1)} fusion(f32[256,8,128]{2,0,1:T(8,128)} %get-tuple-element.144, bf16[256,8,16,128]{3,0,2,1:T(8,128)(2,1)} %bitcast.92, bf16[8,16,128,128]{3,2,1,0:T(8,128)(2,1)} %get-tuple-element.156, f32[8]{0:T(128)S(1)} %compare_convert_fusion.3), kind=kOutput, calls=%fused_computation.11.clone.1 | convolution fusion | flops 1074528256 | bytes 14680096 | tf_op jit(solution)/shard_map/while/body/eval_jaxpr/cbkj,bkij->cbi/dot_general | solution.py:23
  320.5 1.3 collective-permute-start
  322.4 5.8 %collective-permute-start.1 = (bf16[256,4,128]{2,0,1:T(8,128)(2,1)S(1)}, bf16[256,4,128]{2,0,1:T(8,128)(2,1)}, u32[]{:S(2)}, u32[]{:S(2)}) collective-permute-start(bf16[256,4,128]{2,0,1:T(8,128)(2,1)S(1)} %bitcast.95), channel_id=1, source_target_pairs={{0,4},{4,8},{8,12},{12,16},{16,20},{20,24},{24,28},{1,5},{5,9},{9,... | collective-permute-start | bytes 786440 | tf_op jit(solution)/shard_map/while/body/eval_jaxpr/ppermute | solution.py:12
  328.9 2.5 collective-permute-done
  331.4 5.8 %collective-permute-done.1 = bf16[256,4,128]{2,0,1:T(8,128)(2,1)} collective-permute-done((bf16[256,4,128]{2,0,1:T(8,128)(2,1)S(1)}, bf16[256,4,128]{2,0,1:T(8,128)(2,1)}, u32[]{:S(2)}, u32[]{:S(2)}) %collective-permute-start.1) | collective-permute-done | bytes 262176 | tf_op jit(solution)/shard_map/while/body/eval_jaxpr/ppermute | solution.py:12
  337.2 1.2 pad_maximum_fusion.3
  338.4 6.6 %gather_fusion.2 = bf16[128,256,128]{2,1,0:T(8,128)(2,1)} fusion(bf16[256,16,128]{2,0,1:T(8,128)(2,1)S(1)} %pad_maximum_fusion.3, s32[1024]{0:T(1024)S(1)} %pad_clamp_fusion.9), kind=kCustom, calls=%fused_computation.2.clone.clone.1 | custom fusion | bytes 16777728 | tf_op jit(solution)/shard_map/while/body/eval_jaxpr/gather | solution.py:22
  345.0 7.2 %fusion.27 = f32[256,8,128]{2,0,1:T(8,128)S(1)} fusion(f32[256,8,128]{2,0,1:T(8,128)} %get-tuple-element.144, bf16[256,8,16,128]{3,0,2,1:T(8,128)(2,1)} %bitcast.92, bf16[8,16,128,128]{3,2,1,0:T(8,128)(2,1)} %get-tuple-element.156, f32[8]{0:T(128)S(1)} %compare_convert_fusion.3), kind=kOutput, calls=%fused_computation.11.clone.1 | convolution fusion | flops 1074528256 | bytes 14680096 | tf_op jit(solution)/shard_map/while/body/eval_jaxpr/cbkj,bkij->cbi/dot_general | solution.py:23
  354.0 1.3 collective-permute-start
  355.9 5.8 %collective-permute-start.1 = (bf16[256,4,128]{2,0,1:T(8,128)(2,1)S(1)}, bf16[256,4,128]{2,0,1:T(8,128)(2,1)}, u32[]{:S(2)}, u32[]{:S(2)}) collective-permute-start(bf16[256,4,128]{2,0,1:T(8,128)(2,1)S(1)} %bitcast.95), channel_id=1, source_target_pairs={{0,4},{4,8},{8,12},{12,16},{16,20},{20,24},{24,28},{1,5},{5,9},{9,... | collective-permute-start | bytes 786440 | tf_op jit(solution)/shard_map/while/body/eval_jaxpr/ppermute | solution.py:12
  362.5 2.5 collective-permute-done
  365.0 5.8 %collective-permute-done.1 = bf16[256,4,128]{2,0,1:T(8,128)(2,1)} collective-permute-done((bf16[256,4,128]{2,0,1:T(8,128)(2,1)S(1)}, bf16[256,4,128]{2,0,1:T(8,128)(2,1)}, u32[]{:S(2)}, u32[]{:S(2)}) %collective-permute-start.1) | collective-permute-done | bytes 262176 | tf_op jit(solution)/shard_map/while/body/eval_jaxpr/ppermute | solution.py:12
  372.0 6.6 %gather_fusion.2 = bf16[128,256,128]{2,1,0:T(8,128)(2,1)} fusion(bf16[256,16,128]{2,0,1:T(8,128)(2,1)S(1)} %pad_maximum_fusion.3, s32[1024]{0:T(1024)S(1)} %pad_clamp_fusion.9), kind=kCustom, calls=%fused_computation.2.clone.clone.1 | custom fusion | bytes 16777728 | tf_op jit(solution)/shard_map/while/body/eval_jaxpr/gather | solution.py:22
  378.6 7.2 %fusion.27 = f32[256,8,128]{2,0,1:T(8,128)S(1)} fusion(f32[256,8,128]{2,0,1:T(8,128)} %get-tuple-element.144, bf16[256,8,16,128]{3,0,2,1:T(8,128)(2,1)} %bitcast.92, bf16[8,16,128,128]{3,2,1,0:T(8,128)(2,1)} %get-tuple-element.156, f32[8]{0:T(128)S(1)} %compare_convert_fusion.3), kind=kOutput, calls=%fused_computation.11.clone.1 | convolution fusion | flops 1074528256 | bytes 14680096 | tf_op jit(solution)/shard_map/while/body/eval_jaxpr/cbkj,bkij->cbi/dot_general | solution.py:23
  (144 shorter events, 41.5 us)
Async XLA Ops:
  6.5 39.6 %copy-start = (f32[1024,256]{1,0:T(8,128)S(1)}, f32[1024,256]{1,0:T(8,128)}, u32[]{:S(2)}) copy-start(f32[1024,256]{1,0:T(8,128)} %param.9) | copy-start | bytes 3145732
  6.5 55.4 %copy-start.2 = (s32[8,16]{1,0:T(8,128)S(1)}, s32[8,16]{1,0:T(8,128)}, u32[]{:S(2)}) copy-start(s32[8,16]{1,0:T(8,128)} %param.11) | copy-start | bytes 1540
  6.5 39.6 %all-gather.2.cloned.1.call-start = ((), (), s32[]{:S(2)}) async-start(), calls=%async_computation | async-start | bytes 5242880 | tf_op jit(solution)/shard_map/all_gather | solution.py:32
  56.7 14.9 %collective-permute-start.2 = (bf16[256,4,128]{2,0,1:T(8,128)(2,1)S(1)}, bf16[256,4,128]{2,0,1:T(8,128)(2,1)S(1)}, u32[]{:S(2)}, u32[]{:S(2)}) collective-permute-start(bf16[256,4,128]{2,0,1:T(8,128)(2,1)S(1)} %bitcast.96), channel_id=1, source_target_pairs={{0,4},{4,8},{8,12},{12,16},{16,20},{20,24},{24,28},{1,5},{5,9},{9,... | collective-permute-start | bytes 786440 | tf_op jit(solution)/shard_map/ppermute | solution.py:12
  60.7 10.9 %collective-permute-start.3 = (bf16[256,4,128]{2,0,1:T(8,128)(2,1)S(1)}, bf16[256,4,128]{2,0,1:T(8,128)(2,1)S(1)}, u32[]{:S(2)}, u32[]{:S(2)}) collective-permute-start(bf16[256,4,128]{2,0,1:T(8,128)(2,1)S(1)} %bitcast.97), channel_id=1, source_target_pairs={{4,0},{8,4},{12,8},{16,12},{20,16},{24,20},{28,24},{5,1},{9,5},{13... | collective-permute-start | bytes 786440 | tf_op jit(solution)/shard_map/ppermute | solution.py:12
  78.3 6.9 %copy-start.3 = (s32[1,2,4]{2,1,0:T(2,128)S(1)}, s32[1,2,4]{2,1,0:T(2,128)}, u32[]{:S(2)}) copy-start(s32[1,2,4]{2,1,0:T(2,128)} %param.12) | copy-start | bytes 100
  85.3 10.9 %copy-start.1 = (bf16[256,8,128]{2,0,1:T(8,128)(2,1)}, bf16[256,8,128]{2,0,1:T(8,128)(2,1)S(1)}, u32[]{:S(2)}) copy-start(bf16[256,8,128]{2,0,1:T(8,128)(2,1)S(1)} %convert_element_type.26) | copy-start | bytes 1572868 | tf_op jit(solution)/shard_map/while
  86.0 10.2 %collective-permute-start = (bf16[256,4,128]{2,0,1:T(8,128)(2,1)S(1)}, bf16[256,4,128]{2,0,1:T(8,128)(2,1)S(1)}, u32[]{:S(2)}, u32[]{:S(2)}) collective-permute-start(bf16[256,4,128]{2,0,1:T(8,128)(2,1)S(1)} %bitcast.94), channel_id=1, source_target_pairs={{4,0},{8,4},{12,8},{16,12},{20,16},{24,20},{28,24},{5,1},{9,5},{13... | collective-permute-start | bytes 786440 | tf_op jit(solution)/shard_map/while/body/eval_jaxpr/ppermute | solution.py:12
  87.9 14.5 %collective-permute-start.1 = (bf16[256,4,128]{2,0,1:T(8,128)(2,1)S(1)}, bf16[256,4,128]{2,0,1:T(8,128)(2,1)}, u32[]{:S(2)}, u32[]{:S(2)}) collective-permute-start(bf16[256,4,128]{2,0,1:T(8,128)(2,1)S(1)} %bitcast.95), channel_id=1, source_target_pairs={{0,4},{4,8},{8,12},{12,16},{16,20},{20,24},{24,28},{1,5},{5,9},{9,... | collective-permute-start | bytes 786440 | tf_op jit(solution)/shard_map/while/body/eval_jaxpr/ppermute | solution.py:12
  118.5 11.6 %copy-start.1 = (bf16[256,8,128]{2,0,1:T(8,128)(2,1)}, bf16[256,8,128]{2,0,1:T(8,128)(2,1)S(1)}, u32[]{:S(2)}) copy-start(bf16[256,8,128]{2,0,1:T(8,128)(2,1)S(1)} %convert_element_type.26) | copy-start | bytes 1572868 | tf_op jit(solution)/shard_map/while
  119.1 11.0 %collective-permute-start = (bf16[256,4,128]{2,0,1:T(8,128)(2,1)S(1)}, bf16[256,4,128]{2,0,1:T(8,128)(2,1)S(1)}, u32[]{:S(2)}, u32[]{:S(2)}) collective-permute-start(bf16[256,4,128]{2,0,1:T(8,128)(2,1)S(1)} %bitcast.94), channel_id=1, source_target_pairs={{4,0},{8,4},{12,8},{16,12},{20,16},{24,20},{28,24},{5,1},{9,5},{13... | collective-permute-start | bytes 786440 | tf_op jit(solution)/shard_map/while/body/eval_jaxpr/ppermute | solution.py:12
  121.1 14.8 %collective-permute-start.1 = (bf16[256,4,128]{2,0,1:T(8,128)(2,1)S(1)}, bf16[256,4,128]{2,0,1:T(8,128)(2,1)}, u32[]{:S(2)}, u32[]{:S(2)}) collective-permute-start(bf16[256,4,128]{2,0,1:T(8,128)(2,1)S(1)} %bitcast.95), channel_id=1, source_target_pairs={{0,4},{4,8},{8,12},{12,16},{16,20},{20,24},{24,28},{1,5},{5,9},{9,... | collective-permute-start | bytes 786440 | tf_op jit(solution)/shard_map/while/body/eval_jaxpr/ppermute | solution.py:12
  152.1 11.6 %copy-start.1 = (bf16[256,8,128]{2,0,1:T(8,128)(2,1)}, bf16[256,8,128]{2,0,1:T(8,128)(2,1)S(1)}, u32[]{:S(2)}) copy-start(bf16[256,8,128]{2,0,1:T(8,128)(2,1)S(1)} %convert_element_type.26) | copy-start | bytes 1572868 | tf_op jit(solution)/shard_map/while
  152.7 11.0 %collective-permute-start = (bf16[256,4,128]{2,0,1:T(8,128)(2,1)S(1)}, bf16[256,4,128]{2,0,1:T(8,128)(2,1)S(1)}, u32[]{:S(2)}, u32[]{:S(2)}) collective-permute-start(bf16[256,4,128]{2,0,1:T(8,128)(2,1)S(1)} %bitcast.94), channel_id=1, source_target_pairs={{4,0},{8,4},{12,8},{16,12},{20,16},{24,20},{28,24},{5,1},{9,5},{13... | collective-permute-start | bytes 786440 | tf_op jit(solution)/shard_map/while/body/eval_jaxpr/ppermute | solution.py:12
  154.6 14.8 %collective-permute-start.1 = (bf16[256,4,128]{2,0,1:T(8,128)(2,1)S(1)}, bf16[256,4,128]{2,0,1:T(8,128)(2,1)}, u32[]{:S(2)}, u32[]{:S(2)}) collective-permute-start(bf16[256,4,128]{2,0,1:T(8,128)(2,1)S(1)} %bitcast.95), channel_id=1, source_target_pairs={{0,4},{4,8},{8,12},{12,16},{16,20},{20,24},{24,28},{1,5},{5,9},{9,... | collective-permute-start | bytes 786440 | tf_op jit(solution)/shard_map/while/body/eval_jaxpr/ppermute | solution.py:12
  185.6 11.6 %copy-start.1 = (bf16[256,8,128]{2,0,1:T(8,128)(2,1)}, bf16[256,8,128]{2,0,1:T(8,128)(2,1)S(1)}, u32[]{:S(2)}) copy-start(bf16[256,8,128]{2,0,1:T(8,128)(2,1)S(1)} %convert_element_type.26) | copy-start | bytes 1572868 | tf_op jit(solution)/shard_map/while
  186.2 11.0 %collective-permute-start = (bf16[256,4,128]{2,0,1:T(8,128)(2,1)S(1)}, bf16[256,4,128]{2,0,1:T(8,128)(2,1)S(1)}, u32[]{:S(2)}, u32[]{:S(2)}) collective-permute-start(bf16[256,4,128]{2,0,1:T(8,128)(2,1)S(1)} %bitcast.94), channel_id=1, source_target_pairs={{4,0},{8,4},{12,8},{16,12},{20,16},{24,20},{28,24},{5,1},{9,5},{13... | collective-permute-start | bytes 786440 | tf_op jit(solution)/shard_map/while/body/eval_jaxpr/ppermute | solution.py:12
  188.2 14.8 %collective-permute-start.1 = (bf16[256,4,128]{2,0,1:T(8,128)(2,1)S(1)}, bf16[256,4,128]{2,0,1:T(8,128)(2,1)}, u32[]{:S(2)}, u32[]{:S(2)}) collective-permute-start(bf16[256,4,128]{2,0,1:T(8,128)(2,1)S(1)} %bitcast.95), channel_id=1, source_target_pairs={{0,4},{4,8},{8,12},{12,16},{16,20},{20,24},{24,28},{1,5},{5,9},{9,... | collective-permute-start | bytes 786440 | tf_op jit(solution)/shard_map/while/body/eval_jaxpr/ppermute | solution.py:12
  219.2 11.6 %copy-start.1 = (bf16[256,8,128]{2,0,1:T(8,128)(2,1)}, bf16[256,8,128]{2,0,1:T(8,128)(2,1)S(1)}, u32[]{:S(2)}) copy-start(bf16[256,8,128]{2,0,1:T(8,128)(2,1)S(1)} %convert_element_type.26) | copy-start | bytes 1572868 | tf_op jit(solution)/shard_map/while
  219.8 11.0 %collective-permute-start = (bf16[256,4,128]{2,0,1:T(8,128)(2,1)S(1)}, bf16[256,4,128]{2,0,1:T(8,128)(2,1)S(1)}, u32[]{:S(2)}, u32[]{:S(2)}) collective-permute-start(bf16[256,4,128]{2,0,1:T(8,128)(2,1)S(1)} %bitcast.94), channel_id=1, source_target_pairs={{4,0},{8,4},{12,8},{16,12},{20,16},{24,20},{28,24},{5,1},{9,5},{13... | collective-permute-start | bytes 786440 | tf_op jit(solution)/shard_map/while/body/eval_jaxpr/ppermute | solution.py:12
  221.7 14.8 %collective-permute-start.1 = (bf16[256,4,128]{2,0,1:T(8,128)(2,1)S(1)}, bf16[256,4,128]{2,0,1:T(8,128)(2,1)}, u32[]{:S(2)}, u32[]{:S(2)}) collective-permute-start(bf16[256,4,128]{2,0,1:T(8,128)(2,1)S(1)} %bitcast.95), channel_id=1, source_target_pairs={{0,4},{4,8},{8,12},{12,16},{16,20},{20,24},{24,28},{1,5},{5,9},{9,... | collective-permute-start | bytes 786440 | tf_op jit(solution)/shard_map/while/body/eval_jaxpr/ppermute | solution.py:12
  252.7 11.6 %copy-start.1 = (bf16[256,8,128]{2,0,1:T(8,128)(2,1)}, bf16[256,8,128]{2,0,1:T(8,128)(2,1)S(1)}, u32[]{:S(2)}) copy-start(bf16[256,8,128]{2,0,1:T(8,128)(2,1)S(1)} %convert_element_type.26) | copy-start | bytes 1572868 | tf_op jit(solution)/shard_map/while
  253.3 11.0 %collective-permute-start = (bf16[256,4,128]{2,0,1:T(8,128)(2,1)S(1)}, bf16[256,4,128]{2,0,1:T(8,128)(2,1)S(1)}, u32[]{:S(2)}, u32[]{:S(2)}) collective-permute-start(bf16[256,4,128]{2,0,1:T(8,128)(2,1)S(1)} %bitcast.94), channel_id=1, source_target_pairs={{4,0},{8,4},{12,8},{16,12},{20,16},{24,20},{28,24},{5,1},{9,5},{13... | collective-permute-start | bytes 786440 | tf_op jit(solution)/shard_map/while/body/eval_jaxpr/ppermute | solution.py:12
  255.3 14.8 %collective-permute-start.1 = (bf16[256,4,128]{2,0,1:T(8,128)(2,1)S(1)}, bf16[256,4,128]{2,0,1:T(8,128)(2,1)}, u32[]{:S(2)}, u32[]{:S(2)}) collective-permute-start(bf16[256,4,128]{2,0,1:T(8,128)(2,1)S(1)} %bitcast.95), channel_id=1, source_target_pairs={{0,4},{4,8},{8,12},{12,16},{16,20},{20,24},{24,28},{1,5},{5,9},{9,... | collective-permute-start | bytes 786440 | tf_op jit(solution)/shard_map/while/body/eval_jaxpr/ppermute | solution.py:12
  286.3 11.6 %copy-start.1 = (bf16[256,8,128]{2,0,1:T(8,128)(2,1)}, bf16[256,8,128]{2,0,1:T(8,128)(2,1)S(1)}, u32[]{:S(2)}) copy-start(bf16[256,8,128]{2,0,1:T(8,128)(2,1)S(1)} %convert_element_type.26) | copy-start | bytes 1572868 | tf_op jit(solution)/shard_map/while
  286.9 11.0 %collective-permute-start = (bf16[256,4,128]{2,0,1:T(8,128)(2,1)S(1)}, bf16[256,4,128]{2,0,1:T(8,128)(2,1)S(1)}, u32[]{:S(2)}, u32[]{:S(2)}) collective-permute-start(bf16[256,4,128]{2,0,1:T(8,128)(2,1)S(1)} %bitcast.94), channel_id=1, source_target_pairs={{4,0},{8,4},{12,8},{16,12},{20,16},{24,20},{28,24},{5,1},{9,5},{13... | collective-permute-start | bytes 786440 | tf_op jit(solution)/shard_map/while/body/eval_jaxpr/ppermute | solution.py:12
  288.8 14.8 %collective-permute-start.1 = (bf16[256,4,128]{2,0,1:T(8,128)(2,1)S(1)}, bf16[256,4,128]{2,0,1:T(8,128)(2,1)}, u32[]{:S(2)}, u32[]{:S(2)}) collective-permute-start(bf16[256,4,128]{2,0,1:T(8,128)(2,1)S(1)} %bitcast.95), channel_id=1, source_target_pairs={{0,4},{4,8},{8,12},{12,16},{16,20},{20,24},{24,28},{1,5},{5,9},{9,... | collective-permute-start | bytes 786440 | tf_op jit(solution)/shard_map/while/body/eval_jaxpr/ppermute | solution.py:12
  319.8 11.6 %copy-start.1 = (bf16[256,8,128]{2,0,1:T(8,128)(2,1)}, bf16[256,8,128]{2,0,1:T(8,128)(2,1)S(1)}, u32[]{:S(2)}) copy-start(bf16[256,8,128]{2,0,1:T(8,128)(2,1)S(1)} %convert_element_type.26) | copy-start | bytes 1572868 | tf_op jit(solution)/shard_map/while
  320.5 11.0 %collective-permute-start = (bf16[256,4,128]{2,0,1:T(8,128)(2,1)S(1)}, bf16[256,4,128]{2,0,1:T(8,128)(2,1)S(1)}, u32[]{:S(2)}, u32[]{:S(2)}) collective-permute-start(bf16[256,4,128]{2,0,1:T(8,128)(2,1)S(1)} %bitcast.94), channel_id=1, source_target_pairs={{4,0},{8,4},{12,8},{16,12},{20,16},{24,20},{28,24},{5,1},{9,5},{13... | collective-permute-start | bytes 786440 | tf_op jit(solution)/shard_map/while/body/eval_jaxpr/ppermute | solution.py:12
  322.4 14.8 %collective-permute-start.1 = (bf16[256,4,128]{2,0,1:T(8,128)(2,1)S(1)}, bf16[256,4,128]{2,0,1:T(8,128)(2,1)}, u32[]{:S(2)}, u32[]{:S(2)}) collective-permute-start(bf16[256,4,128]{2,0,1:T(8,128)(2,1)S(1)} %bitcast.95), channel_id=1, source_target_pairs={{0,4},{4,8},{8,12},{12,16},{16,20},{20,24},{24,28},{1,5},{5,9},{9,... | collective-permute-start | bytes 786440 | tf_op jit(solution)/shard_map/while/body/eval_jaxpr/ppermute | solution.py:12
  353.4 11.6 %copy-start.1 = (bf16[256,8,128]{2,0,1:T(8,128)(2,1)}, bf16[256,8,128]{2,0,1:T(8,128)(2,1)S(1)}, u32[]{:S(2)}) copy-start(bf16[256,8,128]{2,0,1:T(8,128)(2,1)S(1)} %convert_element_type.26) | copy-start | bytes 1572868 | tf_op jit(solution)/shard_map/while
  354.0 11.0 %collective-permute-start = (bf16[256,4,128]{2,0,1:T(8,128)(2,1)S(1)}, bf16[256,4,128]{2,0,1:T(8,128)(2,1)S(1)}, u32[]{:S(2)}, u32[]{:S(2)}) collective-permute-start(bf16[256,4,128]{2,0,1:T(8,128)(2,1)S(1)} %bitcast.94), channel_id=1, source_target_pairs={{4,0},{8,4},{12,8},{16,12},{20,16},{24,20},{28,24},{5,1},{9,5},{13... | collective-permute-start | bytes 786440 | tf_op jit(solution)/shard_map/while/body/eval_jaxpr/ppermute | solution.py:12
  355.9 14.8 %collective-permute-start.1 = (bf16[256,4,128]{2,0,1:T(8,128)(2,1)S(1)}, bf16[256,4,128]{2,0,1:T(8,128)(2,1)}, u32[]{:S(2)}, u32[]{:S(2)}) collective-permute-start(bf16[256,4,128]{2,0,1:T(8,128)(2,1)S(1)} %bitcast.95), channel_id=1, source_target_pairs={{0,4},{4,8},{8,12},{12,16},{16,20},{20,24},{24,28},{1,5},{5,9},{9,... | collective-permute-start | bytes 786440 | tf_op jit(solution)/shard_map/while/body/eval_jaxpr/ppermute | solution.py:12
Sparse Core Ops, SparseCore 0:
  8.9 37.1 all-gather.1
where the time goes:
time: 396 us; the launch traced here: 395 us
  waiting for transfers between devices  122 us (31%)
  local copies, waits for them, and re-layouts  89 us (22%)
  matrix products  80.4 us (20%)
  starting transfers between devices  68.7 us (17%)
  other arithmetic  19.9 us (5%)
  between operations  14.1 us (4%)
    ppermute x20, waiting for transfers between devices, passed_along(): return lax.ppermute(x, axis, pairs)  83.5 us
    dot_general x10, matrix products, apply_blocks(): jnp.einsum('cbkj,bkij->cbi', picked, blocks, preferred_element_type=jnp.f...  71.6 us
    ppermute x20, starting transfers between devices, passed_along(): return lax.ppermute(x, axis, pairs)  68.7 us
    gather x10, local copies, waits for them, and re-layouts, apply_blocks(): picked = source[:, cols, :]  65.7 us
    all_gather x1, waiting for transfers between devices, body(): lax.all_gather(vectors, 'col', axis=0, tiled=True)  37.4 us
    concatenate x10, other arithmetic, apply_blocks(): source = jnp.concatenate([from_prev, lowered, from_next], axis=1)  11.2 us
    while x36, local copies, waits for them, and re-layouts  9.43 us
    dot_general x1, matrix products, body(): lax.dot_general(rotation, lax.all_gather(vectors, 'col', axis=0, tiled=Tr...  8.72 us
  transfers between devices with their start and end apart: 21, of which 20 were waited for; matrix products, arithmetic and copies ran while one was open for 3% of the time, Pallas kernels for 0%

commit v1 on v0

--- a/solution.py
+++ b/solution.py
@@ -4,6 +4,18 @@
 from jax.sharding import PartitionSpec as P
 
 STEPS = 10
+
+
+def collect(array, axis, dim):
+    ways, here = (lax.axis_size(axis), lax.axis_index(axis))
+    grown, reach = (array, 1)
+    while reach < ways:
+        theirs = lax.ppermute(grown, axis, [(d, d ^ reach) for d in range(ways)])
+        mine_first = jnp.concatenate([grown, theirs], axis=dim)
+        theirs_first = jnp.concatenate([theirs, grown], axis=dim)
+        grown = jnp.where(here & reach == 0, mine_first, theirs_first)
+        reach = 2 * reach
+    return grown
 
 
 def passed_along(x, axis, by):
@@ -29,7 +41,7 @@
     width = blocks.shape[2]
     panel = lax.dot_general(
         rotation,
-        lax.all_gather(vectors, "col", axis=0, tiled=True),
+        collect(vectors, "col", 0),
         (((0,), (1,)), ((), ())),
         precision=lax.Precision.HIGHEST,
         preferred_element_type=jnp.float32,

time: 396 us -> 396 us (level)
  between operations: 14.1 us -> 0.77 us
  waiting for transfers between devices: 122 us -> 129 us
    ppermute x0 -> x2, waiting for transfers between devices: none -> 48 us  [collect(): theirs = lax.ppermute(grown, axis, [(d, d ^ reach) for d in range(ways)])]
    all_gather x1 -> x0, waiting for transfers between devices: 37.4 us -> none  [body(): lax.all_gather(vectors, 'col', axis=0, tiled=True)]
  transfers between devices with their start and end apart: 21 -> 22, of which waited for: 20 -> 21; matrix products, arithmetic and copies ran while one was open for 3% -> 3% of each run, Pallas kernels for 0% -> 0%
where the time goes in v1:
time: 396 us; the launch traced here: 393 us
  waiting for transfers between devices  129 us (33%)
  local copies, waits for them, and re-layouts  90.4 us (23%)
  matrix products  78.3 us (20%)
  starting transfers between devices  72.4 us (18%)
  other arithmetic  21.8 us (6%)
    ppermute x20, waiting for transfers between devices, passed_along(): return lax.ppermute(x, axis, pairs)  80.8 us
    dot_general x10, matrix products, apply_blocks(): jnp.einsum('cbkj,bkij->cbi', picked, blocks, preferred_element_type=jnp.f...  71.6 us
    ppermute x20, starting transfers between devices, passed_along(): return lax.ppermute(x, axis, pairs)  69 us
    gather x10, local copies, waits for them, and re-layouts, apply_blocks(): picked = source[:, cols, :]  65.5 us
    ppermute x2, waiting for transfers between devices, collect(): theirs = lax.ppermute(grown, axis, [(d, d ^ reach) for d in range(ways)])  48 us
    concatenate x10, other arithmetic, apply_blocks(): source = jnp.concatenate([from_prev, lowered, from_next], axis=1)  11.2 us
    while x36, local copies, waits for them, and re-layouts  9.43 us
  transfers between devices with their start and end apart: 22, of which 21 were waited for; matrix products, arithmetic and copies ran while one was open for 3% of the time, Pallas kernels for 0%

profile of v1, /device:TPU:0, one launch (start us, length us, event | category | flops | bytes accessed | tf_op | source)
XLA Modules:
  0.0 393.4 jit_solution(2413244800748667238)
XLA Ops:
  0.5 2.6 collective-permute-done.2
  3.1 2.7 maximum_select_fusion.2
  5.8 2.9 collective-permute-start.3
  9.4 45.3 %collective-permute-done.3 = f32[512,1024]{1,0:T(8,128)} collective-permute-done((f32[512,1024]{1,0:T(8,128)S(1)}, f32[512,1024]{1,0:T(8,128)}, u32[]{:S(2)}, u32[]{:S(2)}) %collective-permute-start.3) | collective-permute-done | bytes 2097184 | tf_op jit(solution)/shard_map/ppermute | solution.py:13
  54.8 6.6 %fusion.8 = f32[1024,256]{1,0:T(8,128)} fusion(f32[1024,256]{1,0:T(8,128)S(1)} %copy-done, f32[512,1024]{1,0:T(8,128)} %collective-permute-done.3, f32[512,1024]{1,0:T(8,128)S(1)} %maximum_select_fusion.2, pred[]{:T(512)S(6)} %eq.6), kind=kOutput, calls=%fused_computation.23 | convolution fusion | flops 3224371200 | bytes 6291457 | tf_op jit(solution)/shard_map/dot_general | solution.py:42
  61.4 1.6 copy.7
  64.8 3.6 collective-permute-start.4
  69.0 1.3 collective-permute-start.5
  70.4 8.6 %collective-permute-done.4 = bf16[256,4,128]{2,0,1:T(8,128)(2,1)S(1)} collective-permute-done((bf16[256,4,128]{2,0,1:T(8,128)(2,1)S(1)}, bf16[256,4,128]{2,0,1:T(8,128)(2,1)S(1)}, u32[]{:S(2)}, u32[]{:S(2)}) %collective-permute-start.4) | collective-permute-done | bytes 262176 | tf_op jit(solution)/shard_map/ppermute | solution.py:24
  79.1 6.6 %gather_fusion.5 = bf16[128,256,128]{2,1,0:T(8,128)(2,1)} fusion(bf16[256,16,128]{2,0,1:T(8,128)(2,1)S(1)} %pad_maximum_fusion.1, s32[1024]{0:T(1024)S(1)} %pad_clamp_fusion.3), kind=kCustom, calls=%fused_computation.5 | custom fusion | bytes 16777728 | tf_op jit(solution)/shard_map/gather | solution.py:34
  85.7 6.9 %fusion.16 = f32[256,8,128]{2,0,1:T(8,128)S(1)} fusion(bf16[256,8,16,128]{3,0,2,1:T(8,128)(2,1)} %bitcast.90, bf16[8,16,128,128]{3,2,1,0:T(8,128)(2,1)} %param.10, f32[8]{0:T(128)S(1)} %compare_convert_fusion.1), kind=kOutput, calls=%fused_computation.33 | convolution fusion | flops 1074003968 | bytes 13631520 | tf_op jit(solution)/shard_map/cbkj,bkij->cbi/dot_general | solution.py:35
  92.6 299.7 %while.13 = (s32[]{:T(128)}, f32[256,8,128]{2,0,1:T(8,128)}, f32[256,8,128]{2,0,1:T(8,128)S(1)}, s32[1,2,4]{2,1,0:T(2,128)S(1)}, s32[8,16]{1,0:T(8,128)S(1)}, /*...) while((s32[]{:T(128)}, f32[256,8,128]{2,0,1:T(8,128)}, f32[256,8,128]{2,0,1:T(8,128)S(1)}, ...), condition=%wide.region_1.2_spmd.clone, body=%wide.region_0.1_spmd.clone.sunk | while | flops 1075842432 | bytes 44580228 | solution.py:58
  93.3 1.3 collective-permute-start
  95.2 5.7 %collective-permute-start.1 = (bf16[256,4,128]{2,0,1:T(8,128)(2,1)S(1)}, bf16[256,4,128]{2,0,1:T(8,128)(2,1)}, u32[]{:S(2)}, u32[]{:S(2)}) collective-permute-start(bf16[256,4,128]{2,0,1:T(8,128)(2,1)S(1)} %bitcast.92), channel_id=1, source_target_pairs={{0,4},{4,8},{8,12},{12,16},{16,20},{20,24},{24,28},{1,5},{5,9},{9,... | collective-permute-start | bytes 786440 | tf_op jit(solution)/shard_map/while/body/eval_jaxpr/ppermute | solution.py:24
  102.1 6.8 %collective-permute-done.1 = bf16[256,4,128]{2,0,1:T(8,128)(2,1)} collective-permute-done((bf16[256,4,128]{2,0,1:T(8,128)(2,1)S(1)}, bf16[256,4,128]{2,0,1:T(8,128)(2,1)}, u32[]{:S(2)}, u32[]{:S(2)}) %collective-permute-start.1) | collective-permute-done | bytes 262176 | tf_op jit(solution)/shard_map/while/body/eval_jaxpr/ppermute | solution.py:24
  110.1 6.6 %gather_fusion.2 = bf16[128,256,128]{2,1,0:T(8,128)(2,1)} fusion(bf16[256,16,128]{2,0,1:T(8,128)(2,1)S(1)} %pad_maximum_fusion.3, s32[1024]{0:T(1024)S(1)} %pad_clamp_fusion.9), kind=kCustom, calls=%fused_computation.2.clone.clone.1 | custom fusion | bytes 16777728 | tf_op jit(solution)/shard_map/while/body/eval_jaxpr/gather | solution.py:34
  116.7 7.2 %fusion.34 = f32[256,8,128]{2,0,1:T(8,128)S(1)} fusion(f32[256,8,128]{2,0,1:T(8,128)} %get-tuple-element.144, bf16[256,8,16,128]{3,0,2,1:T(8,128)(2,1)} %bitcast.89, bf16[8,16,128,128]{3,2,1,0:T(8,128)(2,1)} %get-tuple-element.156, f32[8]{0:T(128)S(1)} %compare_convert_fusion.3), kind=kOutput, calls=%fused_computation.11.clone.1 | convolution fusion | flops 1074528256 | bytes 14680096 | tf_op jit(solution)/shard_map/while/body/eval_jaxpr/cbkj,bkij->cbi/dot_general | solution.py:35
  125.7 1.3 collective-permute-start
  127.6 5.8 %collective-permute-start.1 = (bf16[256,4,128]{2,0,1:T(8,128)(2,1)S(1)}, bf16[256,4,128]{2,0,1:T(8,128)(2,1)}, u32[]{:S(2)}, u32[]{:S(2)}) collective-permute-start(bf16[256,4,128]{2,0,1:T(8,128)(2,1)S(1)} %bitcast.92), channel_id=1, source_target_pairs={{0,4},{4,8},{8,12},{12,16},{16,20},{20,24},{24,28},{1,5},{5,9},{9,... | collective-permute-start | bytes 786440 | tf_op jit(solution)/shard_map/while/body/eval_jaxpr/ppermute | solution.py:24
  134.2 1.6 collective-permute-done
  135.8 5.8 %collective-permute-done.1 = bf16[256,4,128]{2,0,1:T(8,128)(2,1)} collective-permute-done((bf16[256,4,128]{2,0,1:T(8,128)(2,1)S(1)}, bf16[256,4,128]{2,0,1:T(8,128)(2,1)}, u32[]{:S(2)}, u32[]{:S(2)}) %collective-permute-start.1) | collective-permute-done | bytes 262176 | tf_op jit(solution)/shard_map/while/body/eval_jaxpr/ppermute | solution.py:24
  142.8 6.6 %gather_fusion.2 = bf16[128,256,128]{2,1,0:T(8,128)(2,1)} fusion(bf16[256,16,128]{2,0,1:T(8,128)(2,1)S(1)} %pad_maximum_fusion.3, s32[1024]{0:T(1024)S(1)} %pad_clamp_fusion.9), kind=kCustom, calls=%fused_computation.2.clone.clone.1 | custom fusion | bytes 16777728 | tf_op jit(solution)/shard_map/while/body/eval_jaxpr/gather | solution.py:34
  149.3 7.2 %fusion.34 = f32[256,8,128]{2,0,1:T(8,128)S(1)} fusion(f32[256,8,128]{2,0,1:T(8,128)} %get-tuple-element.144, bf16[256,8,16,128]{3,0,2,1:T(8,128)(2,1)} %bitcast.89, bf16[8,16,128,128]{3,2,1,0:T(8,128)(2,1)} %get-tuple-element.156, f32[8]{0:T(128)S(1)} %compare_convert_fusion.3), kind=kOutput, calls=%fused_computation.11.clone.1 | convolution fusion | flops 1074528256 | bytes 14680096 | tf_op jit(solution)/shard_map/while/body/eval_jaxpr/cbkj,bkij->cbi/dot_general | solution.py:35
  158.3 1.3 collective-permute-start
  160.2 5.8 %collective-permute-start.1 = (bf16[256,4,128]{2,0,1:T(8,128)(2,1)S(1)}, bf16[256,4,128]{2,0,1:T(8,128)(2,1)}, u32[]{:S(2)}, u32[]{:S(2)}) collective-permute-start(bf16[256,4,128]{2,0,1:T(8,128)(2,1)S(1)} %bitcast.92), channel_id=1, source_target_pairs={{0,4},{4,8},{8,12},{12,16},{16,20},{20,24},{24,28},{1,5},{5,9},{9,... | collective-permute-start | bytes 786440 | tf_op jit(solution)/shard_map/while/body/eval_jaxpr/ppermute | solution.py:24
  166.8 2.5 collective-permute-done
  169.3 5.8 %collective-permute-done.1 = bf16[256,4,128]{2,0,1:T(8,128)(2,1)} collective-permute-done((bf16[256,4,128]{2,0,1:T(8,128)(2,1)S(1)}, bf16[256,4,128]{2,0,1:T(8,128)(2,1)}, u32[]{:S(2)}, u32[]{:S(2)}) %collective-permute-start.1) | collective-permute-done | bytes 262176 | tf_op jit(solution)/shard_map/while/body/eval_jaxpr/ppermute | solution.py:24
  176.3 6.6 %gather_fusion.2 = bf16[128,256,128]{2,1,0:T(8,128)(2,1)} fusion(bf16[256,16,128]{2,0,1:T(8,128)(2,1)S(1)} %pad_maximum_fusion.3, s32[1024]{0:T(1024)S(1)} %pad_clamp_fusion.9), kind=kCustom, calls=%fused_computation.2.clone.clone.1 | custom fusion | bytes 16777728 | tf_op jit(solution)/shard_map/while/body/eval_jaxpr/gather | solution.py:34
  182.9 7.2 %fusion.34 = f32[256,8,128]{2,0,1:T(8,128)S(1)} fusion(f32[256,8,128]{2,0,1:T(8,128)} %get-tuple-element.144, bf16[256,8,16,128]{3,0,2,1:T(8,128)(2,1)} %bitcast.89, bf16[8,16,128,128]{3,2,1,0:T(8,128)(2,1)} %get-tuple-element.156, f32[8]{0:T(128)S(1)} %compare_convert_fusion.3), kind=kOutput, calls=%fused_computation.11.clone.1 | convolution fusion | flops 1074528256 | bytes 14680096 | tf_op jit(solution)/shard_map/while/body/eval_jaxpr/cbkj,bkij->cbi/dot_general | solution.py:35
  191.9 1.3 collective-permute-start
  193.8 5.8 %collective-permute-start.1 = (bf16[256,4,128]{2,0,1:T(8,128)(2,1)S(1)}, bf16[256,4,128]{2,0,1:T(8,128)(2,1)}, u32[]{:S(2)}, u32[]{:S(2)}) collective-permute-start(bf16[256,4,128]{2,0,1:T(8,128)(2,1)S(1)} %bitcast.92), channel_id=1, source_target_pairs={{0,4},{4,8},{8,12},{12,16},{16,20},{20,24},{24,28},{1,5},{5,9},{9,... | collective-permute-start | bytes 786440 | tf_op jit(solution)/shard_map/while/body/eval_jaxpr/ppermute | solution.py:24
  200.4 2.5 collective-permute-done
  202.8 5.8 %collective-permute-done.1 = bf16[256,4,128]{2,0,1:T(8,128)(2,1)} collective-permute-done((bf16[256,4,128]{2,0,1:T(8,128)(2,1)S(1)}, bf16[256,4,128]{2,0,1:T(8,128)(2,1)}, u32[]{:S(2)}, u32[]{:S(2)}) %collective-permute-start.1) | collective-permute-done | bytes 262176 | tf_op jit(solution)/shard_map/while/body/eval_jaxpr/ppermute | solution.py:24
  209.8 6.6 %gather_fusion.2 = bf16[128,256,128]{2,1,0:T(8,128)(2,1)} fusion(bf16[256,16,128]{2,0,1:T(8,128)(2,1)S(1)} %pad_maximum_fusion.3, s32[1024]{0:T(1024)S(1)} %pad_clamp_fusion.9), kind=kCustom, calls=%fused_computation.2.clone.clone.1 | custom fusion | bytes 16777728 | tf_op jit(solution)/shard_map/while/body/eval_jaxpr/gather | solution.py:34
  216.4 7.2 %fusion.34 = f32[256,8,128]{2,0,1:T(8,128)S(1)} fusion(f32[256,8,128]{2,0,1:T(8,128)} %get-tuple-element.144, bf16[256,8,16,128]{3,0,2,1:T(8,128)(2,1)} %bitcast.89, bf16[8,16,128,128]{3,2,1,0:T(8,128)(2,1)} %get-tuple-element.156, f32[8]{0:T(128)S(1)} %compare_convert_fusion.3), kind=kOutput, calls=%fused_computation.11.clone.1 | convolution fusion | flops 1074528256 | bytes 14680096 | tf_op jit(solution)/shard_map/while/body/eval_jaxpr/cbkj,bkij->cbi/dot_general | solution.py:35
  225.4 1.3 collective-permute-start
  227.3 5.8 %collective-permute-start.1 = (bf16[256,4,128]{2,0,1:T(8,128)(2,1)S(1)}, bf16[256,4,128]{2,0,1:T(8,128)(2,1)}, u32[]{:S(2)}, u32[]{:S(2)}) collective-permute-start(bf16[256,4,128]{2,0,1:T(8,128)(2,1)S(1)} %bitcast.92), channel_id=1, source_target_pairs={{0,4},{4,8},{8,12},{12,16},{16,20},{20,24},{24,28},{1,5},{5,9},{9,... | collective-permute-start | bytes 786440 | tf_op jit(solution)/shard_map/while/body/eval_jaxpr/ppermute | solution.py:24
  233.9 2.5 collective-permute-done
  236.4 5.8 %collective-permute-done.1 = bf16[256,4,128]{2,0,1:T(8,128)(2,1)} collective-permute-done((bf16[256,4,128]{2,0,1:T(8,128)(2,1)S(1)}, bf16[256,4,128]{2,0,1:T(8,128)(2,1)}, u32[]{:S(2)}, u32[]{:S(2)}) %collective-permute-start.1) | collective-permute-done | bytes 262176 | tf_op jit(solution)/shard_map/while/body/eval_jaxpr/ppermute | solution.py:24
  243.4 6.6 %gather_fusion.2 = bf16[128,256,128]{2,1,0:T(8,128)(2,1)} fusion(bf16[256,16,128]{2,0,1:T(8,128)(2,1)S(1)} %pad_maximum_fusion.3, s32[1024]{0:T(1024)S(1)} %pad_clamp_fusion.9), kind=kCustom, calls=%fused_computation.2.clone.clone.1 | custom fusion | bytes 16777728 | tf_op jit(solution)/shard_map/while/body/eval_jaxpr/gather | solution.py:34
  249.9 7.2 %fusion.34 = f32[256,8,128]{2,0,1:T(8,128)S(1)} fusion(f32[256,8,128]{2,0,1:T(8,128)} %get-tuple-element.144, bf16[256,8,16,128]{3,0,2,1:T(8,128)(2,1)} %bitcast.89, bf16[8,16,128,128]{3,2,1,0:T(8,128)(2,1)} %get-tuple-element.156, f32[8]{0:T(128)S(1)} %compare_convert_fusion.3), kind=kOutput, calls=%fused_computation.11.clone.1 | convolution fusion | flops 1074528256 | bytes 14680096 | tf_op jit(solution)/shard_map/while/body/eval_jaxpr/cbkj,bkij->cbi/dot_general | solution.py:35
  258.9 1.3 collective-permute-start
  260.8 5.8 %collective-permute-start.1 = (bf16[256,4,128]{2,0,1:T(8,128)(2,1)S(1)}, bf16[256,4,128]{2,0,1:T(8,128)(2,1)}, u32[]{:S(2)}, u32[]{:S(2)}) collective-permute-start(bf16[256,4,128]{2,0,1:T(8,128)(2,1)S(1)} %bitcast.92), channel_id=1, source_target_pairs={{0,4},{4,8},{8,12},{12,16},{16,20},{20,24},{24,28},{1,5},{5,9},{9,... | collective-permute-start | bytes 786440 | tf_op jit(solution)/shard_map/while/body/eval_jaxpr/ppermute | solution.py:24
  267.4 2.5 collective-permute-done
  269.9 5.8 %collective-permute-done.1 = bf16[256,4,128]{2,0,1:T(8,128)(2,1)} collective-permute-done((bf16[256,4,128]{2,0,1:T(8,128)(2,1)S(1)}, bf16[256,4,128]{2,0,1:T(8,128)(2,1)}, u32[]{:S(2)}, u32[]{:S(2)}) %collective-permute-start.1) | collective-permute-done | bytes 262176 | tf_op jit(solution)/shard_map/while/body/eval_jaxpr/ppermute | solution.py:24
  276.9 6.6 %gather_fusion.2 = bf16[128,256,128]{2,1,0:T(8,128)(2,1)} fusion(bf16[256,16,128]{2,0,1:T(8,128)(2,1)S(1)} %pad_maximum_fusion.3, s32[1024]{0:T(1024)S(1)} %pad_clamp_fusion.9), kind=kCustom, calls=%fused_computation.2.clone.clone.1 | custom fusion | bytes 16777728 | tf_op jit(solution)/shard_map/while/body/eval_jaxpr/gather | solution.py:34
  283.5 7.2 %fusion.34 = f32[256,8,128]{2,0,1:T(8,128)S(1)} fusion(f32[256,8,128]{2,0,1:T(8,128)} %get-tuple-element.144, bf16[256,8,16,128]{3,0,2,1:T(8,128)(2,1)} %bitcast.89, bf16[8,16,128,128]{3,2,1,0:T(8,128)(2,1)} %get-tuple-element.156, f32[8]{0:T(128)S(1)} %compare_convert_fusion.3), kind=kOutput, calls=%fused_computation.11.clone.1 | convolution fusion | flops 1074528256 | bytes 14680096 | tf_op jit(solution)/shard_map/while/body/eval_jaxpr/cbkj,bkij->cbi/dot_general | solution.py:35
  292.5 1.3 collective-permute-start
  294.4 5.8 %collective-permute-start.1 = (bf16[256,4,128]{2,0,1:T(8,128)(2,1)S(1)}, bf16[256,4,128]{2,0,1:T(8,128)(2,1)}, u32[]{:S(2)}, u32[]{:S(2)}) collective-permute-start(bf16[256,4,128]{2,0,1:T(8,128)(2,1)S(1)} %bitcast.92), channel_id=1, source_target_pairs={{0,4},{4,8},{8,12},{12,16},{16,20},{20,24},{24,28},{1,5},{5,9},{9,... | collective-permute-start | bytes 786440 | tf_op jit(solution)/shard_map/while/body/eval_jaxpr/ppermute | solution.py:24
  301.0 2.5 collective-permute-done
  303.4 5.8 %collective-permute-done.1 = bf16[256,4,128]{2,0,1:T(8,128)(2,1)} collective-permute-done((bf16[256,4,128]{2,0,1:T(8,128)(2,1)S(1)}, bf16[256,4,128]{2,0,1:T(8,128)(2,1)}, u32[]{:S(2)}, u32[]{:S(2)}) %collective-permute-start.1) | collective-permute-done | bytes 262176 | tf_op jit(solution)/shard_map/while/body/eval_jaxpr/ppermute | solution.py:24
  310.4 6.6 %gather_fusion.2 = bf16[128,256,128]{2,1,0:T(8,128)(2,1)} fusion(bf16[256,16,128]{2,0,1:T(8,128)(2,1)S(1)} %pad_maximum_fusion.3, s32[1024]{0:T(1024)S(1)} %pad_clamp_fusion.9), kind=kCustom, calls=%fused_computation.2.clone.clone.1 | custom fusion | bytes 16777728 | tf_op jit(solution)/shard_map/while/body/eval_jaxpr/gather | solution.py:34
  317.0 7.2 %fusion.34 = f32[256,8,128]{2,0,1:T(8,128)S(1)} fusion(f32[256,8,128]{2,0,1:T(8,128)} %get-tuple-element.144, bf16[256,8,16,128]{3,0,2,1:T(8,128)(2,1)} %bitcast.89, bf16[8,16,128,128]{3,2,1,0:T(8,128)(2,1)} %get-tuple-element.156, f32[8]{0:T(128)S(1)} %compare_convert_fusion.3), kind=kOutput, calls=%fused_computation.11.clone.1 | convolution fusion | flops 1074528256 | bytes 14680096 | tf_op jit(solution)/shard_map/while/body/eval_jaxpr/cbkj,bkij->cbi/dot_general | solution.py:35
  327.9 5.8 %collective-permute-start.1 = (bf16[256,4,128]{2,0,1:T(8,128)(2,1)S(1)}, bf16[256,4,128]{2,0,1:T(8,128)(2,1)}, u32[]{:S(2)}, u32[]{:S(2)}) collective-permute-start(bf16[256,4,128]{2,0,1:T(8,128)(2,1)S(1)} %bitcast.92), channel_id=1, source_target_pairs={{0,4},{4,8},{8,12},{12,16},{16,20},{20,24},{24,28},{1,5},{5,9},{9,... | collective-permute-start | bytes 786440 | tf_op jit(solution)/shard_map/while/body/eval_jaxpr/ppermute | solution.py:24
  334.5 2.5 collective-permute-done
  337.0 5.8 %collective-permute-done.1 = bf16[256,4,128]{2,0,1:T(8,128)(2,1)} collective-permute-done((bf16[256,4,128]{2,0,1:T(8,128)(2,1)S(1)}, bf16[256,4,128]{2,0,1:T(8,128)(2,1)}, u32[]{:S(2)}, u32[]{:S(2)}) %collective-permute-start.1) | collective-permute-done | bytes 262176 | tf_op jit(solution)/shard_map/while/body/eval_jaxpr/ppermute | solution.py:24
  344.0 6.6 %gather_fusion.2 = bf16[128,256,128]{2,1,0:T(8,128)(2,1)} fusion(bf16[256,16,128]{2,0,1:T(8,128)(2,1)S(1)} %pad_maximum_fusion.3, s32[1024]{0:T(1024)S(1)} %pad_clamp_fusion.9), kind=kCustom, calls=%fused_computation.2.clone.clone.1 | custom fusion | bytes 16777728 | tf_op jit(solution)/shard_map/while/body/eval_jaxpr/gather | solution.py:34
  350.5 7.2 %fusion.34 = f32[256,8,128]{2,0,1:T(8,128)S(1)} fusion(f32[256,8,128]{2,0,1:T(8,128)} %get-tuple-element.144, bf16[256,8,16,128]{3,0,2,1:T(8,128)(2,1)} %bitcast.89, bf16[8,16,128,128]{3,2,1,0:T(8,128)(2,1)} %get-tuple-element.156, f32[8]{0:T(128)S(1)} %compare_convert_fusion.3), kind=kOutput, calls=%fused_computation.11.clone.1 | convolution fusion | flops 1074528256 | bytes 14680096 | tf_op jit(solution)/shard_map/while/body/eval_jaxpr/cbkj,bkij->cbi/dot_general | solution.py:35
  359.5 1.3 collective-permute-start
  361.4 5.8 %collective-permute-start.1 = (bf16[256,4,128]{2,0,1:T(8,128)(2,1)S(1)}, bf16[256,4,128]{2,0,1:T(8,128)(2,1)}, u32[]{:S(2)}, u32[]{:S(2)}) collective-permute-start(bf16[256,4,128]{2,0,1:T(8,128)(2,1)S(1)} %bitcast.92), channel_id=1, source_target_pairs={{0,4},{4,8},{8,12},{12,16},{16,20},{20,24},{24,28},{1,5},{5,9},{9,... | collective-permute-start | bytes 786440 | tf_op jit(solution)/shard_map/while/body/eval_jaxpr/ppermute | solution.py:24
  368.0 2.5 collective-permute-done
  370.5 5.8 %collective-permute-done.1 = bf16[256,4,128]{2,0,1:T(8,128)(2,1)} collective-permute-done((bf16[256,4,128]{2,0,1:T(8,128)(2,1)S(1)}, bf16[256,4,128]{2,0,1:T(8,128)(2,1)}, u32[]{:S(2)}, u32[]{:S(2)}) %collective-permute-start.1) | collective-permute-done | bytes 262176 | tf_op jit(solution)/shard_map/while/body/eval_jaxpr/ppermute | solution.py:24
  377.5 6.6 %gather_fusion.2 = bf16[128,256,128]{2,1,0:T(8,128)(2,1)} fusion(bf16[256,16,128]{2,0,1:T(8,128)(2,1)S(1)} %pad_maximum_fusion.3, s32[1024]{0:T(1024)S(1)} %pad_clamp_fusion.9), kind=kCustom, calls=%fused_computation.2.clone.clone.1 | custom fusion | bytes 16777728 | tf_op jit(solution)/shard_map/while/body/eval_jaxpr/gather | solution.py:34
  384.1 7.2 %fusion.34 = f32[256,8,128]{2,0,1:T(8,128)S(1)} fusion(f32[256,8,128]{2,0,1:T(8,128)} %get-tuple-element.144, bf16[256,8,16,128]{3,0,2,1:T(8,128)(2,1)} %bitcast.89, bf16[8,16,128,128]{3,2,1,0:T(8,128)(2,1)} %get-tuple-element.156, f32[8]{0:T(128)S(1)} %compare_convert_fusion.3), kind=kOutput, calls=%fused_computation.11.clone.1 | convolution fusion | flops 1074528256 | bytes 14680096 | tf_op jit(solution)/shard_map/while/body/eval_jaxpr/cbkj,bkij->cbi/dot_general | solution.py:35
  (147 shorter events, 44.6 us)
Async XLA Ops:
  0.0 54.8 %copy-start = (f32[1024,256]{1,0:T(8,128)S(1)}, f32[1024,256]{1,0:T(8,128)}, u32[]{:S(2)}) copy-start(f32[1024,256]{1,0:T(8,128)} %param.9) | copy-start | bytes 3145732
  0.0 9.4 %copy-start.3 = (s32[1,2,4]{2,1,0:T(2,128)S(1)}, s32[1,2,4]{2,1,0:T(2,128)}, u32[]{:S(2)}) copy-start(s32[1,2,4]{2,1,0:T(2,128)} %param.12) | copy-start | bytes 100
  0.0 3.1 collective-permute-start.2
  5.8 49.0 %collective-permute-start.3 = (f32[512,1024]{1,0:T(8,128)S(1)}, f32[512,1024]{1,0:T(8,128)}, u32[]{:S(2)}, u32[]{:S(2)}) collective-permute-start(f32[512,1024]{1,0:T(8,128)S(1)} %maximum_select_fusion.2), channel_id=1, source_target_pairs={{0,2},{1,3},{2,0},{3,1},{4,6},{5,7},{6,4},{7,5},{8,10},{9,11},{10,... | collective-permute-start | bytes 6291464 | tf_op jit(solution)/shard_map/ppermute | solution.py:13
  61.4 8.9 %copy-start.2 = (s32[8,16]{1,0:T(8,128)S(1)}, s32[8,16]{1,0:T(8,128)}, u32[]{:S(2)}) copy-start(s32[8,16]{1,0:T(8,128)} %param.11) | copy-start | bytes 1540
  64.8 14.2 %collective-permute-start.4 = (bf16[256,4,128]{2,0,1:T(8,128)(2,1)S(1)}, bf16[256,4,128]{2,0,1:T(8,128)(2,1)S(1)}, u32[]{:S(2)}, u32[]{:S(2)}) collective-permute-start(bf16[256,4,128]{2,0,1:T(8,128)(2,1)S(1)} %bitcast.94), channel_id=1, source_target_pairs={{0,4},{4,8},{8,12},{12,16},{16,20},{20,24},{24,28},{1,5},{5,9},{9,... | collective-permute-start | bytes 786440 | tf_op jit(solution)/shard_map/ppermute | solution.py:24
  69.0 10.0 %collective-permute-start.5 = (bf16[256,4,128]{2,0,1:T(8,128)(2,1)S(1)}, bf16[256,4,128]{2,0,1:T(8,128)(2,1)S(1)}, u32[]{:S(2)}, u32[]{:S(2)}) collective-permute-start(bf16[256,4,128]{2,0,1:T(8,128)(2,1)S(1)} %bitcast.95), channel_id=1, source_target_pairs={{4,0},{8,4},{12,8},{16,12},{20,16},{24,20},{28,24},{5,1},{9,5},{13... | collective-permute-start | bytes 786440 | tf_op jit(solution)/shard_map/ppermute | solution.py:24
  92.7 9.4 %copy-start.1 = (bf16[256,8,128]{2,0,1:T(8,128)(2,1)}, bf16[256,8,128]{2,0,1:T(8,128)(2,1)S(1)}, u32[]{:S(2)}) copy-start(bf16[256,8,128]{2,0,1:T(8,128)(2,1)S(1)} %convert_element_type.26) | copy-start | bytes 1572868 | tf_op jit(solution)/shard_map/while
  93.3 8.7 %collective-permute-start = (bf16[256,4,128]{2,0,1:T(8,128)(2,1)S(1)}, bf16[256,4,128]{2,0,1:T(8,128)(2,1)S(1)}, u32[]{:S(2)}, u32[]{:S(2)}) collective-permute-start(bf16[256,4,128]{2,0,1:T(8,128)(2,1)S(1)} %bitcast.91), channel_id=1, source_target_pairs={{4,0},{8,4},{12,8},{16,12},{20,16},{24,20},{28,24},{5,1},{9,5},{13... | collective-permute-start | bytes 786440 | tf_op jit(solution)/shard_map/while/body/eval_jaxpr/ppermute | solution.py:24
  95.2 13.7 %collective-permute-start.1 = (bf16[256,4,128]{2,0,1:T(8,128)(2,1)S(1)}, bf16[256,4,128]{2,0,1:T(8,128)(2,1)}, u32[]{:S(2)}, u32[]{:S(2)}) collective-permute-start(bf16[256,4,128]{2,0,1:T(8,128)(2,1)S(1)} %bitcast.92), channel_id=1, source_target_pairs={{0,4},{4,8},{8,12},{12,16},{16,20},{20,24},{24,28},{1,5},{5,9},{9,... | collective-permute-start | bytes 786440 | tf_op jit(solution)/shard_map/while/body/eval_jaxpr/ppermute | solution.py:24
  125.1 10.7 %copy-start.1 = (bf16[256,8,128]{2,0,1:T(8,128)(2,1)}, bf16[256,8,128]{2,0,1:T(8,128)(2,1)S(1)}, u32[]{:S(2)}) copy-start(bf16[256,8,128]{2,0,1:T(8,128)(2,1)S(1)} %convert_element_type.26) | copy-start | bytes 1572868 | tf_op jit(solution)/shard_map/while
  125.7 10.1 %collective-permute-start = (bf16[256,4,128]{2,0,1:T(8,128)(2,1)S(1)}, bf16[256,4,128]{2,0,1:T(8,128)(2,1)S(1)}, u32[]{:S(2)}, u32[]{:S(2)}) collective-permute-start(bf16[256,4,128]{2,0,1:T(8,128)(2,1)S(1)} %bitcast.91), channel_id=1, source_target_pairs={{4,0},{8,4},{12,8},{16,12},{20,16},{24,20},{28,24},{5,1},{9,5},{13... | collective-permute-start | bytes 786440 | tf_op jit(solution)/shard_map/while/body/eval_jaxpr/ppermute | solution.py:24
  127.6 14.0 %collective-permute-start.1 = (bf16[256,4,128]{2,0,1:T(8,128)(2,1)S(1)}, bf16[256,4,128]{2,0,1:T(8,128)(2,1)}, u32[]{:S(2)}, u32[]{:S(2)}) collective-permute-start(bf16[256,4,128]{2,0,1:T(8,128)(2,1)S(1)} %bitcast.92), channel_id=1, source_target_pairs={{0,4},{4,8},{8,12},{12,16},{16,20},{20,24},{24,28},{1,5},{5,9},{9,... | collective-permute-start | bytes 786440 | tf_op jit(solution)/shard_map/while/body/eval_jaxpr/ppermute | solution.py:24
  157.7 11.6 %copy-start.1 = (bf16[256,8,128]{2,0,1:T(8,128)(2,1)}, bf16[256,8,128]{2,0,1:T(8,128)(2,1)S(1)}, u32[]{:S(2)}) copy-start(bf16[256,8,128]{2,0,1:T(8,128)(2,1)S(1)} %convert_element_type.26) | copy-start | bytes 1572868 | tf_op jit(solution)/shard_map/while
  158.3 11.0 %collective-permute-start = (bf16[256,4,128]{2,0,1:T(8,128)(2,1)S(1)}, bf16[256,4,128]{2,0,1:T(8,128)(2,1)S(1)}, u32[]{:S(2)}, u32[]{:S(2)}) collective-permute-start(bf16[256,4,128]{2,0,1:T(8,128)(2,1)S(1)} %bitcast.91), channel_id=1, source_target_pairs={{4,0},{8,4},{12,8},{16,12},{20,16},{24,20},{28,24},{5,1},{9,5},{13... | collective-permute-start | bytes 786440 | tf_op jit(solution)/shard_map/while/body/eval_jaxpr/ppermute | solution.py:24
  160.2 14.8 %collective-permute-start.1 = (bf16[256,4,128]{2,0,1:T(8,128)(2,1)S(1)}, bf16[256,4,128]{2,0,1:T(8,128)(2,1)}, u32[]{:S(2)}, u32[]{:S(2)}) collective-permute-start(bf16[256,4,128]{2,0,1:T(8,128)(2,1)S(1)} %bitcast.92), channel_id=1, source_target_pairs={{0,4},{4,8},{8,12},{12,16},{16,20},{20,24},{24,28},{1,5},{5,9},{9,... | collective-permute-start | bytes 786440 | tf_op jit(solution)/shard_map/while/body/eval_jaxpr/ppermute | solution.py:24
  191.2 11.6 %copy-start.1 = (bf16[256,8,128]{2,0,1:T(8,128)(2,1)}, bf16[256,8,128]{2,0,1:T(8,128)(2,1)S(1)}, u32[]{:S(2)}) copy-start(bf16[256,8,128]{2,0,1:T(8,128)(2,1)S(1)} %convert_element_type.26) | copy-start | bytes 1572868 | tf_op jit(solution)/shard_map/while
  191.9 11.0 %collective-permute-start = (bf16[256,4,128]{2,0,1:T(8,128)(2,1)S(1)}, bf16[256,4,128]{2,0,1:T(8,128)(2,1)S(1)}, u32[]{:S(2)}, u32[]{:S(2)}) collective-permute-start(bf16[256,4,128]{2,0,1:T(8,128)(2,1)S(1)} %bitcast.91), channel_id=1, source_target_pairs={{4,0},{8,4},{12,8},{16,12},{20,16},{24,20},{28,24},{5,1},{9,5},{13... | collective-permute-start | bytes 786440 | tf_op jit(solution)/shard_map/while/body/eval_jaxpr/ppermute | solution.py:24
  193.8 14.8 %collective-permute-start.1 = (bf16[256,4,128]{2,0,1:T(8,128)(2,1)S(1)}, bf16[256,4,128]{2,0,1:T(8,128)(2,1)}, u32[]{:S(2)}, u32[]{:S(2)}) collective-permute-start(bf16[256,4,128]{2,0,1:T(8,128)(2,1)S(1)} %bitcast.92), channel_id=1, source_target_pairs={{0,4},{4,8},{8,12},{12,16},{16,20},{20,24},{24,28},{1,5},{5,9},{9,... | collective-permute-start | bytes 786440 | tf_op jit(solution)/shard_map/while/body/eval_jaxpr/ppermute | solution.py:24
  224.8 11.6 %copy-start.1 = (bf16[256,8,128]{2,0,1:T(8,128)(2,1)}, bf16[256,8,128]{2,0,1:T(8,128)(2,1)S(1)}, u32[]{:S(2)}) copy-start(bf16[256,8,128]{2,0,1:T(8,128)(2,1)S(1)} %convert_element_type.26) | copy-start | bytes 1572868 | tf_op jit(solution)/shard_map/while
  225.4 11.0 %collective-permute-start = (bf16[256,4,128]{2,0,1:T(8,128)(2,1)S(1)}, bf16[256,4,128]{2,0,1:T(8,128)(2,1)S(1)}, u32[]{:S(2)}, u32[]{:S(2)}) collective-permute-start(bf16[256,4,128]{2,0,1:T(8,128)(2,1)S(1)} %bitcast.91), channel_id=1, source_target_pairs={{4,0},{8,4},{12,8},{16,12},{20,16},{24,20},{28,24},{5,1},{9,5},{13... | collective-permute-start | bytes 786440 | tf_op jit(solution)/shard_map/while/body/eval_jaxpr/ppermute | solution.py:24
  227.3 14.8 %collective-permute-start.1 = (bf16[256,4,128]{2,0,1:T(8,128)(2,1)S(1)}, bf16[256,4,128]{2,0,1:T(8,128)(2,1)}, u32[]{:S(2)}, u32[]{:S(2)}) collective-permute-start(bf16[256,4,128]{2,0,1:T(8,128)(2,1)S(1)} %bitcast.92), channel_id=1, source_target_pairs={{0,4},{4,8},{8,12},{12,16},{16,20},{20,24},{24,28},{1,5},{5,9},{9,... | collective-permute-start | bytes 786440 | tf_op jit(solution)/shard_map/while/body/eval_jaxpr/ppermute | solution.py:24
  258.3 11.6 %copy-start.1 = (bf16[256,8,128]{2,0,1:T(8,128)(2,1)}, bf16[256,8,128]{2,0,1:T(8,128)(2,1)S(1)}, u32[]{:S(2)}) copy-start(bf16[256,8,128]{2,0,1:T(8,128)(2,1)S(1)} %convert_element_type.26) | copy-start | bytes 1572868 | tf_op jit(solution)/shard_map/while
  258.9 11.0 %collective-permute-start = (bf16[256,4,128]{2,0,1:T(8,128)(2,1)S(1)}, bf16[256,4,128]{2,0,1:T(8,128)(2,1)S(1)}, u32[]{:S(2)}, u32[]{:S(2)}) collective-permute-start(bf16[256,4,128]{2,0,1:T(8,128)(2,1)S(1)} %bitcast.91), channel_id=1, source_target_pairs={{4,0},{8,4},{12,8},{16,12},{20,16},{24,20},{28,24},{5,1},{9,5},{13... | collective-permute-start | bytes 786440 | tf_op jit(solution)/shard_map/while/body/eval_jaxpr/ppermute | solution.py:24
  260.8 14.8 %collective-permute-start.1 = (bf16[256,4,128]{2,0,1:T(8,128)(2,1)S(1)}, bf16[256,4,128]{2,0,1:T(8,128)(2,1)}, u32[]{:S(2)}, u32[]{:S(2)}) collective-permute-start(bf16[256,4,128]{2,0,1:T(8,128)(2,1)S(1)} %bitcast.92), channel_id=1, source_target_pairs={{0,4},{4,8},{8,12},{12,16},{16,20},{20,24},{24,28},{1,5},{5,9},{9,... | collective-permute-start | bytes 786440 | tf_op jit(solution)/shard_map/while/body/eval_jaxpr/ppermute | solution.py:24
  291.8 11.6 %copy-start.1 = (bf16[256,8,128]{2,0,1:T(8,128)(2,1)}, bf16[256,8,128]{2,0,1:T(8,128)(2,1)S(1)}, u32[]{:S(2)}) copy-start(bf16[256,8,128]{2,0,1:T(8,128)(2,1)S(1)} %convert_element_type.26) | copy-start | bytes 1572868 | tf_op jit(solution)/shard_map/while
  292.5 11.0 %collective-permute-start = (bf16[256,4,128]{2,0,1:T(8,128)(2,1)S(1)}, bf16[256,4,128]{2,0,1:T(8,128)(2,1)S(1)}, u32[]{:S(2)}, u32[]{:S(2)}) collective-permute-start(bf16[256,4,128]{2,0,1:T(8,128)(2,1)S(1)} %bitcast.91), channel_id=1, source_target_pairs={{4,0},{8,4},{12,8},{16,12},{20,16},{24,20},{28,24},{5,1},{9,5},{13... | collective-permute-start | bytes 786440 | tf_op jit(solution)/shard_map/while/body/eval_jaxpr/ppermute | solution.py:24
  294.4 14.8 %collective-permute-start.1 = (bf16[256,4,128]{2,0,1:T(8,128)(2,1)S(1)}, bf16[256,4,128]{2,0,1:T(8,128)(2,1)}, u32[]{:S(2)}, u32[]{:S(2)}) collective-permute-start(bf16[256,4,128]{2,0,1:T(8,128)(2,1)S(1)} %bitcast.92), channel_id=1, source_target_pairs={{0,4},{4,8},{8,12},{12,16},{16,20},{20,24},{24,28},{1,5},{5,9},{9,... | collective-permute-start | bytes 786440 | tf_op jit(solution)/shard_map/while/body/eval_jaxpr/ppermute | solution.py:24
  325.4 11.6 %copy-start.1 = (bf16[256,8,128]{2,0,1:T(8,128)(2,1)}, bf16[256,8,128]{2,0,1:T(8,128)(2,1)S(1)}, u32[]{:S(2)}) copy-start(bf16[256,8,128]{2,0,1:T(8,128)(2,1)S(1)} %convert_element_type.26) | copy-start | bytes 1572868 | tf_op jit(solution)/shard_map/while
  326.0 11.0 %collective-permute-start = (bf16[256,4,128]{2,0,1:T(8,128)(2,1)S(1)}, bf16[256,4,128]{2,0,1:T(8,128)(2,1)S(1)}, u32[]{:S(2)}, u32[]{:S(2)}) collective-permute-start(bf16[256,4,128]{2,0,1:T(8,128)(2,1)S(1)} %bitcast.91), channel_id=1, source_target_pairs={{4,0},{8,4},{12,8},{16,12},{20,16},{24,20},{28,24},{5,1},{9,5},{13... | collective-permute-start | bytes 786440 | tf_op jit(solution)/shard_map/while/body/eval_jaxpr/ppermute | solution.py:24
  327.9 14.8 %collective-permute-start.1 = (bf16[256,4,128]{2,0,1:T(8,128)(2,1)S(1)}, bf16[256,4,128]{2,0,1:T(8,128)(2,1)}, u32[]{:S(2)}, u32[]{:S(2)}) collective-permute-start(bf16[256,4,128]{2,0,1:T(8,128)(2,1)S(1)} %bitcast.92), channel_id=1, source_target_pairs={{0,4},{4,8},{8,12},{12,16},{16,20},{20,24},{24,28},{1,5},{5,9},{9,... | collective-permute-start | bytes 786440 | tf_op jit(solution)/shard_map/while/body/eval_jaxpr/ppermute | solution.py:24
  358.9 11.6 %copy-start.1 = (bf16[256,8,128]{2,0,1:T(8,128)(2,1)}, bf16[256,8,128]{2,0,1:T(8,128)(2,1)S(1)}, u32[]{:S(2)}) copy-start(bf16[256,8,128]{2,0,1:T(8,128)(2,1)S(1)} %convert_element_type.26) | copy-start | bytes 1572868 | tf_op jit(solution)/shard_map/while
  359.5 11.0 %collective-permute-start = (bf16[256,4,128]{2,0,1:T(8,128)(2,1)S(1)}, bf16[256,4,128]{2,0,1:T(8,128)(2,1)S(1)}, u32[]{:S(2)}, u32[]{:S(2)}) collective-permute-start(bf16[256,4,128]{2,0,1:T(8,128)(2,1)S(1)} %bitcast.91), channel_id=1, source_target_pairs={{4,0},{8,4},{12,8},{16,12},{20,16},{24,20},{28,24},{5,1},{9,5},{13... | collective-permute-start | bytes 786440 | tf_op jit(solution)/shard_map/while/body/eval_jaxpr/ppermute | solution.py:24
  361.4 14.8 %collective-permute-start.1 = (bf16[256,4,128]{2,0,1:T(8,128)(2,1)S(1)}, bf16[256,4,128]{2,0,1:T(8,128)(2,1)}, u32[]{:S(2)}, u32[]{:S(2)}) collective-permute-start(bf16[256,4,128]{2,0,1:T(8,128)(2,1)S(1)} %bitcast.92), channel_id=1, source_target_pairs={{0,4},{4,8},{8,12},{12,16},{16,20},{20,24},{24,28},{1,5},{5,9},{9,... | collective-permute-start | bytes 786440 | tf_op jit(solution)/shard_map/while/body/eval_jaxpr/ppermute | solution.py:24
